TPU v7x, 256 devices: a whole 4x4x8 slice. The times are simulated.
256 devices in a mesh: view: 16 (over z, core), blk: 16 (over y, x).
Axes of the slice: x: 4, y: 4, z: 8, core: 2. Of those that a mesh axis runs over, the one named last changes fastest.
Arguments:
- estimate: float32 [256, 128, 128], P('blk'), may hold values from 0.5 to 2
- images: bfloat16 [16, 256, 64, 128], P('view', 'blk'), may hold values from 0.5 to 2
- point_spread: float32 [8, 9, 7, 25], replicated, may hold values from 0.01 to 1
- covered: int32 [8, 16, 4], P(None, 'blk'), may hold values from 0 to 1, as said below
Outputs:
- estimate_next: float32 [256, 128, 128], P('blk')
Inputs may be any that keep to these rules, and one draw needn't show every extreme that they name: For each view and each block layer along the first dimension, the covered blocks are consecutive along the second dimension and at most 3; for every view some block layer has exactly 3.
All inputs are finite; a program needn't handle non-finite values.
Results may differ from a plain program's by a relative error of at most 0.0003.
Values may be sent and summed in bfloat16 or wider, within the bound.
A program may use at most 64 MiB of HBM per device.

v0:
```python
import jax
import jax.numpy as jnp
from jax import lax
from jax.sharding import PartitionSpec as P

BY = 32


def with_halo(cells, sides, width):
    for axis, dim in sides:
        count = lax.axis_size(axis)
        ends = count - 1
        head = lax.slice_in_dim(cells, 0, width, axis=dim)
        tail = lax.slice_in_dim(cells, cells.shape[dim] - width, cells.shape[dim], axis=dim)
        cells = jnp.concatenate(
            [
                lax.ppermute(tail, axis, [(i, (i + 1) % count) for i in range(ends)]),
                cells,
                lax.ppermute(head, axis, [((i + 1) % count, i) for i in range(ends)]),
            ],
            axis=dim,
        )
    return cells


def swapped(block, axis, stride):
    count = lax.axis_size(axis)
    route = []
    for low in range(count):
        high = low | 1 << stride
        if high != low and high < count:
            route += [(low, high), (high, low)]
    return lax.ppermute(block, axis, route)


def merged(part, axis, combine):
    gathered = lax.all_gather(part, axis)

    def take(source):
        return lax.dynamic_index_in_dim(gathered, source, 0, False)

    return lax.fori_loop(
        1, lax.axis_size(axis), lambda source, state: combine(state, take(source)), take(0)
    )


def band_table(kernel, depth):
    taps_x, taps_y, taps_z = kernel.shape
    rim_z = (taps_z - 1) // 2
    shape_three = (taps_z, depth, depth)
    offset = lax.broadcasted_iota(jnp.int32, shape_three, 1) - lax.broadcasted_iota(
        jnp.int32, shape_three, 2
    )
    onehot = (offset + rim_z == lax.broadcasted_iota(jnp.int32, shape_three, 0)).astype(
        jnp.bfloat16
    )
    banded = jnp.einsum("abt,tpz->abpz", kernel, onehot, preferred_element_type=jnp.float32).astype(
        jnp.bfloat16
    )
    return banded.reshape(taps_x, taps_y * depth, depth)


def convolve(padded_part, banded, rows_x, rows_y):
    taps_x = padded_part.shape[0] - rows_x + 1
    taps_y = padded_part.shape[1] - rows_y + 1
    columns = jnp.concatenate(
        [padded_part[:, step_y : step_y + rows_y, :] for step_y in range(taps_y)], axis=2
    )
    output = None
    for shift_x in range(taps_x):
        partial_sum = jnp.dot(
            columns[shift_x : shift_x + rows_x].reshape(rows_x * rows_y, -1),
            banded[shift_x],
            preferred_element_type=jnp.float32,
        )
        output = partial_sum if output is None else output + partial_sum
    return output.reshape(rows_x, rows_y, -1)


def local(estimate, images, point_spread, covered):
    slab_x, width_y, depth = estimate.shape
    share_w = images.shape[2]
    view_count, taps_x, taps_y, taps_z = point_spread.shape
    rim_x, rim_y, rim_z = ((taps_x - 1) // 2, (taps_y - 1) // 2, (taps_z - 1) // 2)
    shares = width_y // share_w
    share_blocks = share_w // BY
    group = lax.axis_index("view")
    view_id = group // shares
    part = group % shares
    y_start = part * share_w
    source = estimate.astype(jnp.bfloat16)
    rimmed = with_halo(source, (("blk", 0),), rim_x)
    padded = jnp.pad(rimmed, ((0, 0), (rim_y, rim_y), (0, 0)))
    spread = lax.dynamic_index_in_dim(point_spread, view_id, 0, keepdims=False)
    kernel = (spread / jnp.sum(spread)).astype(jnp.bfloat16)
    forward = band_table(kernel, depth)
    backward = band_table(kernel[::-1, ::-1, ::-1], depth)
    coverage_row = lax.dynamic_index_in_dim(covered[:, 0, :], view_id, 0, keepdims=False) > 0
    share_cover = lax.dynamic_slice_in_dim(coverage_row, part * share_blocks, share_blocks)
    cell_cover = jnp.repeat(share_cover, BY)[None, :, None]
    image = images[0]
    region = lax.dynamic_slice(
        padded, (0, y_start, 0), (slab_x + 2 * rim_x, share_w + 2 * rim_y, depth)
    )
    blurred = convolve(region, forward, slab_x, share_w)
    quotient = jnp.where(cell_cover, image.astype(jnp.float32) / blurred, 0.0).astype(jnp.bfloat16)
    rim_zeros = jnp.zeros((slab_x, rim_y, depth), jnp.bfloat16)
    edge_rows = jnp.where(part == 0, quotient[:, share_w - rim_y :, :], quotient[:, :rim_y, :])
    partner = swapped(edge_rows, "view", 0)
    lower_rim = jnp.where(part > 0, partner, rim_zeros)
    upper_rim = jnp.where(part < shares - 1, partner, rim_zeros)
    extended = jnp.concatenate([lower_rim, quotient, upper_rim], axis=1)
    quotient_rimmed = with_halo(extended, (("blk", 0),), rim_x)
    correction = convolve(quotient_rimmed, backward, slab_x, share_w)
    share_factor = jnp.where(cell_cover, correction, 1.0)
    n_view = lax.axis_size("view")
    step_x = slab_x // n_view
    rows = share_factor.reshape(n_view, step_x, share_w, depth)
    got = lax.all_to_all(rows, "view", 0, 0)
    got = got.reshape(n_view // shares, shares, step_x, share_w, depth)
    product_rows = jnp.prod(got, axis=0)
    product_rows = jnp.transpose(product_rows, (1, 0, 2, 3)).reshape(step_x, width_y, depth)
    mine = lax.dynamic_slice_in_dim(estimate, group * step_x, step_x, axis=0)
    return lax.all_gather(mine * product_rows, "view", axis=0, tiled=True)


def solution(mesh):
    in_specs = (P("blk", None, None), P("view", "blk", None, None), P(), P(None, "blk", None))
    out_specs = P("blk", None, None)
    return jax.shard_map(local, mesh=mesh, in_specs=in_specs, out_specs=out_specs, check_vma=False)
```

profile of v0, /device:TPU:1, one launch (start us, length us, event | category | flops | bytes accessed | tf_op | source)
XLA Modules:
  0.0 128.2 jit_solution(17272270914108477657)
XLA Ops:
  6.5 1.3 %convert_element_type.30 = bf16[16,128,128]{2,1,0:T(8,128)(2,1)S(1)} convert(f32[16,128,128]{2,1,0:T(8,128)} %param.4) | non-fusion elementwise | flops 262144 | bytes 1572864 | tf_op jit(solution)/shard_map/convert_element_type | solution.py:91
  7.9 4.0 %collective-permute-start = (bf16[4,128,128]{2,1,0:T(8,128)(2,1)S(1)}, bf16[4,128,128]{2,1,0:T(8,128)(2,1)S(1)}, u32[]{:S(2)}, u32[]{:S(2)}) collective-permute-start(bf16[4,128,128]{2,1,0:T(8,128)(2,1)S(1)} %get-tuple-element.44), channel_id=1, source_target_pairs={{0,1},{1,2},{2,3},{3,4},{4,5},{5,6},{6,7},{7,8},{8,9},{9,10},{10,1... | collective-permute-start | bytes 393224 | tf_op jit(solution)/shard_map/ppermute | solution.py:17
  11.8 1.3 %collective-permute-start.1 = (bf16[4,128,128]{2,1,0:T(8,128)(2,1)S(1)}, bf16[4,128,128]{2,1,0:T(8,128)(2,1)S(1)}, u32[]{:S(2)}, u32[]{:S(2)}) collective-permute-start(bf16[4,128,128]{2,1,0:T(8,128)(2,1)S(1)} %get-tuple-element.43), channel_id=1, source_target_pairs={{1,0},{2,1},{3,2},{4,3},{5,4},{6,5},{7,6},{8,7},{9,8},{10,9},{11,1... | collective-permute-start | bytes 393224 | tf_op jit(solution)/shard_map/ppermute | solution.py:19
  13.2 1.6 %fusion.30 = (f32[]{:T(128)}, f32[1,9,7,25]{3,0,2,1:T(1,128)S(1)}) fusion(f32[8,9,7,25]{3,0,2,1:T(8,128)} %param.6, s32[]{:T(128)S(6)} %select_n.62), kind=kLoop, calls=%fused_computation.73 | loop fusion | flops 1574 | bytes 12608 | tf_op jit(solution)/shard_map/reduce_sum | solution.py:95
  14.8 1.5 %fusion.5 = bf16[9,7,128,128]{3,1,2,0:T(8,128)(2,1)S(1)} fusion(f32[1,9,7,25]{3,0,2,1:T(1,128)S(1)} %get-tuple-element.6, f32[]{:T(128)} %get-tuple-element.5), kind=kOutput, calls=%fused_computation.4 | convolution fusion | flops 53873744 | bytes 2070688 | tf_op jit(solution)/shard_map/abt,tpz->abpz/dot_general | solution.py:57
  17.6 0.7 fusion.29
  19.9 3.2 %fusion.32 = (bf16[16,64,896]{2,1,0:T(8,128)(2,1)S(1)}, bf16[16,64,896]{2,1,0:T(8,128)(2,1)S(1)}, bf16[16,64,896]{2,1,0:T(8,128)(2,1)S(1)}, bf16[16,64,896]{2,1,...) fusion(bf16[24,64,896]{2,1,0:T(8,128)(2,1)S(1)} %slice_dynamic-, ...), kind=kLoop, calls=%fused_computation.75 | loop fusion | bytes 33030144 | tf_op jit(solution)/shard_map/slice | solution.py:72
  23.8 0.7 convolution_add_fusion.15
  24.4 0.6 convolution_add_fusion.14
  25.7 0.6 convolution_add_fusion.12
  28.4 0.7 convolution_add_fusion.8
  29.5 1.3 %collective-permute-start.2 = (bf16[16,3,128]{2,1,0:T(4,128)(2,1)S(1)}, bf16[16,3,128]{2,1,0:T(4,128)(2,1)S(1)}, u32[]{:S(2)}, u32[]{:S(2)}) collective-permute-start(bf16[16,3,128]{2,1,0:T(4,128)(2,1)S(1)} %slice_select_fusion), channel_id=1, source_target_pairs={{0,16},{16,0},{32,48},{48,32},{64,80},{80,64},{96,112},{112,96},{1... | collective-permute-start | bytes 36872 | tf_op jit(solution)/shard_map/ppermute | solution.py:33
  30.8 0.9 fusion.8
  31.8 1.3 %collective-permute-start.4 = (bf16[4,70,128]{2,1,0:T(8,128)(2,1)S(1)}, bf16[4,70,128]{2,1,0:T(8,128)(2,1)S(1)}, u32[]{:S(2)}, u32[]{:S(2)}) collective-permute-start(bf16[4,70,128]{2,1,0:T(8,128)(2,1)S(1)} %get-tuple-element.46), channel_id=1, source_target_pairs={{1,0},{2,1},{3,2},{4,3},{5,4},{6,5},{7,6},{8,7},{9,8},{10,9},{11,1... | collective-permute-start | bytes 215048 | tf_op jit(solution)/shard_map/ppermute | solution.py:19
  33.1 4.8 %collective-permute-start.3 = (bf16[4,70,128]{2,1,0:T(8,128)(2,1)S(1)}, bf16[4,70,128]{2,1,0:T(8,128)(2,1)S(1)}, u32[]{:S(2)}, u32[]{:S(2)}) collective-permute-start(bf16[4,70,128]{2,1,0:T(8,128)(2,1)S(1)} %get-tuple-element.45), channel_id=1, source_target_pairs={{0,1},{1,2},{2,3},{3,4},{4,5},{5,6},{6,7},{7,8},{8,9},{9,10},{10,1... | collective-permute-start | bytes 215048 | tf_op jit(solution)/shard_map/ppermute | solution.py:17
  40.3 3.2 %fusion.31 = (bf16[16,64,896]{2,1,0:T(8,128)(2,1)S(1)}, bf16[16,64,896]{2,1,0:T(8,128)(2,1)S(1)}, bf16[16,64,896]{2,1,0:T(8,128)(2,1)S(1)}, bf16[16,64,896]{2,1,...) fusion(bf16[24,64,896]{2,1,0:T(8,128)(2,1)S(1)} %slice_dynamic-, ...), kind=kLoop, calls=%fused_computation.74 | loop fusion | bytes 33030144 | tf_op jit(solution)/shard_map/slice | solution.py:72
  44.2 0.7 convolution_add_fusion.7
  44.8 0.6 convolution_add_fusion.6
  49.4 0.9 broadcast_select_fusion
  50.3 9.6 %all-to-all-start = ((f32[16,1,64,128]{3,2,1,0:T(8,128)}), f32[16,1,64,128]{3,2,1,0:T(8,128)S(1)}, u32[]{:S(2)}, u32[]{:S(2)}) async-start(f32[16,1,64,128]{3,2,1,0:T(8,128)} %broadcast_select_fusion), calls=%async_computation | async-start | bytes 1048576 | tf_op jit(solution)/shard_map/all_to_all | solution.py:119
  60.0 17.3 %all-to-all-done = f32[16,1,64,128]{3,2,1,0:T(8,128)S(1)} async-done(((f32[16,1,64,128]{3,2,1,0:T(8,128)}), f32[16,1,64,128]{3,2,1,0:T(8,128)S(1)}, u32[]{:S(2)}, u32[]{:S(2)}) %all-to-all-start) | async-done | bytes 524320 | tf_op jit(solution)/shard_map/all_to_all | solution.py:119
  77.3 1.5 %bitcast_multiply_fusion = f32[1,128,128]{2,1,0:T(8,128)} fusion(f32[16,128,128]{2,1,0:T(8,128)} %param.4, s32[]{:T(128)S(6)} %select_n.60, f32[1,128,128]{2,1,0:T(8,128)S(1)} %bitcast.144), kind=kLoop, calls=%fused_computation.59 | loop fusion | flops 16384 | bytes 196612 | tf_op jit(solution)/shard_map/mul | solution.py:124
  78.8 40.3 %all-gather.2.cloned.1.call-done = f32[16,128,128]{2,1,0:T(8,128)} async-done(((f32[1,128,128]{2,1,0:T(8,128)}), f32[16,128,128]{2,1,0:T(8,128)}) %all-gather.2.cloned.1.call-update) | async-done | bytes 1048592 | tf_op jit(solution)/shard_map/all_gather | solution.py:124
  119.1 2.3 %copy.70 = f32[16,128,128]{2,1,0:T(8,128)} copy(f32[16,128,128]{2,1,0:T(8,128)} %all-gather.2.cloned.1.call-done) | data formatting | bytes 2097152
  (70 shorter events, 13.5 us)
Async XLA Ops:
  7.9 10.5 %collective-permute-start = (bf16[4,128,128]{2,1,0:T(8,128)(2,1)S(1)}, bf16[4,128,128]{2,1,0:T(8,128)(2,1)S(1)}, u32[]{:S(2)}, u32[]{:S(2)}) collective-permute-start(bf16[4,128,128]{2,1,0:T(8,128)(2,1)S(1)} %get-tuple-element.44), channel_id=1, source_target_pairs={{0,1},{1,2},{2,3},{3,4},{4,5},{5,6},{6,7},{7,8},{8,9},{9,10},{10,1... | collective-permute-start | bytes 393224 | tf_op jit(solution)/shard_map/ppermute | solution.py:17
  11.8 6.6 %collective-permute-start.1 = (bf16[4,128,128]{2,1,0:T(8,128)(2,1)S(1)}, bf16[4,128,128]{2,1,0:T(8,128)(2,1)S(1)}, u32[]{:S(2)}, u32[]{:S(2)}) collective-permute-start(bf16[4,128,128]{2,1,0:T(8,128)(2,1)S(1)} %get-tuple-element.43), channel_id=1, source_target_pairs={{1,0},{2,1},{3,2},{4,3},{5,4},{6,5},{7,6},{8,7},{9,8},{10,9},{11,1... | collective-permute-start | bytes 393224 | tf_op jit(solution)/shard_map/ppermute | solution.py:19
  16.6 0.7 copy-start.1
  28.3 1.0 copy-start
  29.5 2.2 %collective-permute-start.2 = (bf16[16,3,128]{2,1,0:T(4,128)(2,1)S(1)}, bf16[16,3,128]{2,1,0:T(4,128)(2,1)S(1)}, u32[]{:S(2)}, u32[]{:S(2)}) collective-permute-start(bf16[16,3,128]{2,1,0:T(4,128)(2,1)S(1)} %slice_select_fusion), channel_id=1, source_target_pairs={{0,16},{16,0},{32,48},{48,32},{64,80},{80,64},{96,112},{112,96},{1... | collective-permute-start | bytes 36872 | tf_op jit(solution)/shard_map/ppermute | solution.py:33
  31.8 6.7 %collective-permute-start.4 = (bf16[4,70,128]{2,1,0:T(8,128)(2,1)S(1)}, bf16[4,70,128]{2,1,0:T(8,128)(2,1)S(1)}, u32[]{:S(2)}, u32[]{:S(2)}) collective-permute-start(bf16[4,70,128]{2,1,0:T(8,128)(2,1)S(1)} %get-tuple-element.46), channel_id=1, source_target_pairs={{1,0},{2,1},{3,2},{4,3},{5,4},{6,5},{7,6},{8,7},{9,8},{10,9},{11,1... | collective-permute-start | bytes 215048 | tf_op jit(solution)/shard_map/ppermute | solution.py:19
  33.1 6.0 %collective-permute-start.3 = (bf16[4,70,128]{2,1,0:T(8,128)(2,1)S(1)}, bf16[4,70,128]{2,1,0:T(8,128)(2,1)S(1)}, u32[]{:S(2)}, u32[]{:S(2)}) collective-permute-start(bf16[4,70,128]{2,1,0:T(8,128)(2,1)S(1)} %get-tuple-element.45), channel_id=1, source_target_pairs={{0,1},{1,2},{2,3},{3,4},{4,5},{5,6},{6,7},{7,8},{8,9},{9,10},{10,1... | collective-permute-start | bytes 215048 | tf_op jit(solution)/shard_map/ppermute | solution.py:17
  50.3 26.9 %all-to-all-start = ((f32[16,1,64,128]{3,2,1,0:T(8,128)}), f32[16,1,64,128]{3,2,1,0:T(8,128)S(1)}, u32[]{:S(2)}, u32[]{:S(2)}) async-start(f32[16,1,64,128]{3,2,1,0:T(8,128)} %broadcast_select_fusion), calls=%async_computation | async-start | bytes 1048576 | tf_op jit(solution)/shard_map/all_to_all | solution.py:119
  60.0 59.1 %all-gather.2.cloned.1.call-start = ((), (), s32[]{:S(2)}) async-start(), calls=%async_computation.1 | async-start | bytes 1114112 | tf_op jit(solution)/shard_map/all_gather | solution.py:124
Sparse Core Ops, SparseCore 0:
  78.9 40.0 all-gather.1
where the time goes:
time: 129 us; the launch traced here: 128 us
  waiting for transfers between devices  58.2 us (45%)
  starting transfers between devices  22.3 us (17%)
  matrix products  14 us (11%)
  between operations  14 us (11%)
  local copies, waits for them, and re-layouts  12.9 us (10%)
  other arithmetic  6.78 us (5%)
    all_gather x1, waiting for transfers between devices, local(): return lax.all_gather(mine * product_rows, 'view', axis=0, tiled=True)  40.3 us
    all_to_all x1, waiting for transfers between devices, local(): got = lax.all_to_all(rows, 'view', 0, 0)  17.3 us
    dot_general x18, matrix products, convolve(): jnp.dot(columns[shift_x:shift_x + rows_x].reshape(rows_x * rows_y, -1), b...  11.7 us
    all_to_all x1, starting transfers between devices, local(): got = lax.all_to_all(rows, 'view', 0, 0)  9.63 us
    ppermute x2, starting transfers between devices, with_halo(): lax.ppermute(tail, axis, [(i, (i + 1) % count) for i in range(ends)])  8.75 us
    slice x2, local copies, waits for them, and re-layouts, convolve(): columns[shift_x:shift_x + rows_x].reshape(rows_x * rows_y, -1)  6.38 us
    unnamed x17, local copies, waits for them, and re-layouts  4.82 us
    ppermute x2, starting transfers between devices, with_halo(): lax.ppermute(head, axis, [((i + 1) % count, i) for i in range(ends)])  2.58 us
  transfers between devices with their start and end apart: 7, of which 3 were waited for; matrix products, arithmetic and copies ran while one was open for 5% of the time, Pallas kernels for 0%

commit v1 on v0

--- a/solution.py
+++ b/solution.py
@@ -121,7 +121,10 @@
     product_rows = jnp.prod(got, axis=0)
     product_rows = jnp.transpose(product_rows, (1, 0, 2, 3)).reshape(step_x, width_y, depth)
     mine = lax.dynamic_slice_in_dim(estimate, group * step_x, step_x, axis=0)
-    return lax.all_gather(mine * product_rows, "view", axis=0, tiled=True)
+    return jnp.concatenate(
+        lax.all_to_all(jnp.stack([mine * product_rows] * lax.axis_size("view")), "view", 0, 0),
+        axis=0,
+    )
 
 
 def solution(mesh):

time: 129 us -> 110 us (0.85)
  the two profiles are of different devices: /device:TPU:1 before, /device:TPU:25 now
where the time goes in v1:
time: 110 us
  blocking collectives  31.3 us (28%)
  starting transfers between devices  24.4 us (22%)
  waiting for transfers between devices  21.9 us (20%)
  matrix products  14 us (13%)
  local copies, waits for them, and re-layouts  11.7 us (11%)
  other arithmetic  6.15 us (6%)
    all_to_all x1, blocking collectives, local(): lax.all_to_all(jnp.stack([mine * product_rows] * lax.axis_size('view')),...  31.3 us
    all_to_all x1, waiting for transfers between devices, local(): got = lax.all_to_all(rows, 'view', 0, 0)  17.3 us
    dot_general x18, matrix products, convolve(): jnp.dot(columns[shift_x:shift_x + rows_x].reshape(rows_x * rows_y, -1), b...  11.6 us
    all_to_all x1, starting transfers between devices, local(): got = lax.all_to_all(rows, 'view', 0, 0)  10.2 us
    ppermute x2, starting transfers between devices, with_halo(): lax.ppermute(head, axis, [((i + 1) % count, i) for i in range(ends)])  7.67 us
    slice x2, local copies, waits for them, and re-layouts, convolve(): columns[shift_x:shift_x + rows_x].reshape(rows_x * rows_y, -1)  6.38 us
    ppermute x2, starting transfers between devices, with_halo(): lax.ppermute(tail, axis, [(i, (i + 1) % count) for i in range(ends)])  5.22 us
    ppermute x2, waiting for transfers between devices, with_halo(): lax.ppermute(tail, axis, [(i, (i + 1) % count) for i in range(ends)])  4.54 us
  transfers between devices with their start and end apart: 6, of which 2 were waited for; matrix products, arithmetic and copies ran while one was open for 6% of the time, Pallas kernels for 0%

profile of v1, /device:TPU:25, one launch (start us, length us, event | category | flops | bytes accessed | tf_op | source)
XLA Modules:
  0.0 110.0 jit_solution(11583578486269500536)
XLA Ops:
  0.0 1.3 %convert_element_type.30 = bf16[16,128,128]{2,1,0:T(8,128)(2,1)S(1)} convert(f32[16,128,128]{2,1,0:T(8,128)} %param.4) | non-fusion elementwise | flops 262144 | bytes 1572864 | tf_op jit(solution)/shard_map/convert_element_type | solution.py:91
  1.3 3.1 %collective-permute-start = (bf16[4,128,128]{2,1,0:T(8,128)(2,1)S(1)}, bf16[4,128,128]{2,1,0:T(8,128)(2,1)S(1)}, u32[]{:S(2)}, u32[]{:S(2)}) collective-permute-start(bf16[4,128,128]{2,1,0:T(8,128)(2,1)S(1)} %get-tuple-element.44), channel_id=1, source_target_pairs={{0,1},{1,2},{2,3},{3,4},{4,5},{5,6},{6,7},{7,8},{8,9},{9,10},{10,1... | collective-permute-start | bytes 393224 | tf_op jit(solution)/shard_map/ppermute | solution.py:17
  4.5 4.3 %collective-permute-start.1 = (bf16[4,128,128]{2,1,0:T(8,128)(2,1)S(1)}, bf16[4,128,128]{2,1,0:T(8,128)(2,1)S(1)}, u32[]{:S(2)}, u32[]{:S(2)}) collective-permute-start(bf16[4,128,128]{2,1,0:T(8,128)(2,1)S(1)} %get-tuple-element.43), channel_id=1, source_target_pairs={{1,0},{2,1},{3,2},{4,3},{5,4},{6,5},{7,6},{8,7},{9,8},{10,9},{11,1... | collective-permute-start | bytes 393224 | tf_op jit(solution)/shard_map/ppermute | solution.py:19
  8.8 1.6 %fusion.31 = (f32[]{:T(128)}, f32[1,9,7,25]{3,0,2,1:T(1,128)S(1)}) fusion(f32[8,9,7,25]{3,0,2,1:T(8,128)} %param.6, s32[]{:T(128)S(6)} %select_n.62), kind=kLoop, calls=%fused_computation.74 | loop fusion | flops 1574 | bytes 12608 | tf_op jit(solution)/shard_map/reduce_sum | solution.py:95
  10.4 1.5 %fusion.5 = bf16[9,7,128,128]{3,1,2,0:T(8,128)(2,1)S(1)} fusion(f32[1,9,7,25]{3,0,2,1:T(1,128)S(1)} %get-tuple-element.6, f32[]{:T(128)} %get-tuple-element.5), kind=kOutput, calls=%fused_computation.4 | convolution fusion | flops 53873744 | bytes 2070688 | tf_op jit(solution)/shard_map/abt,tpz->abpz/dot_general | solution.py:57
  13.2 0.7 fusion.30
  15.5 3.2 %fusion.33 = (bf16[16,64,896]{2,1,0:T(8,128)(2,1)S(1)}, bf16[16,64,896]{2,1,0:T(8,128)(2,1)S(1)}, bf16[16,64,896]{2,1,0:T(8,128)(2,1)S(1)}, bf16[16,64,896]{2,1,...) fusion(bf16[24,64,896]{2,1,0:T(8,128)(2,1)S(1)} %slice_dynamic-, ...), kind=kLoop, calls=%fused_computation.76 | loop fusion | bytes 33030144 | tf_op jit(solution)/shard_map/slice | solution.py:72
  20.0 0.6 convolution_add_fusion.14
  20.7 0.6 convolution_add_fusion.13
  22.0 0.6 convolution_add_fusion.11
  22.6 0.6 convolution_add_fusion.10
  24.0 0.7 convolution_add_fusion.8
  25.1 1.3 %collective-permute-start.2 = (bf16[16,3,128]{2,1,0:T(4,128)(2,1)S(1)}, bf16[16,3,128]{2,1,0:T(4,128)(2,1)S(1)}, u32[]{:S(2)}, u32[]{:S(2)}) collective-permute-start(bf16[16,3,128]{2,1,0:T(4,128)(2,1)S(1)} %slice_select_fusion), channel_id=1, source_target_pairs={{0,16},{16,0},{32,48},{48,32},{64,80},{80,64},{96,112},{112,96},{1... | collective-permute-start | bytes 36872 | tf_op jit(solution)/shard_map/ppermute | solution.py:33
  26.4 0.9 fusion.8
  27.4 3.4 %collective-permute-start.4 = (bf16[4,70,128]{2,1,0:T(8,128)(2,1)S(1)}, bf16[4,70,128]{2,1,0:T(8,128)(2,1)S(1)}, u32[]{:S(2)}, u32[]{:S(2)}) collective-permute-start(bf16[4,70,128]{2,1,0:T(8,128)(2,1)S(1)} %get-tuple-element.46), channel_id=1, source_target_pairs={{1,0},{2,1},{3,2},{4,3},{5,4},{6,5},{7,6},{8,7},{9,8},{10,9},{11,1... | collective-permute-start | bytes 215048 | tf_op jit(solution)/shard_map/ppermute | solution.py:19
  30.8 2.1 %collective-permute-start.3 = (bf16[4,70,128]{2,1,0:T(8,128)(2,1)S(1)}, bf16[4,70,128]{2,1,0:T(8,128)(2,1)S(1)}, u32[]{:S(2)}, u32[]{:S(2)}) collective-permute-start(bf16[4,70,128]{2,1,0:T(8,128)(2,1)S(1)} %get-tuple-element.45), channel_id=1, source_target_pairs={{0,1},{1,2},{2,3},{3,4},{4,5},{5,6},{6,7},{7,8},{8,9},{9,10},{10,1... | collective-permute-start | bytes 215048 | tf_op jit(solution)/shard_map/ppermute | solution.py:17
  33.5 4.5 %collective-permute-done.3 = bf16[4,70,128]{2,1,0:T(8,128)(2,1)S(1)} collective-permute-done((bf16[4,70,128]{2,1,0:T(8,128)(2,1)S(1)}, bf16[4,70,128]{2,1,0:T(8,128)(2,1)S(1)}, u32[]{:S(2)}, u32[]{:S(2)}) %collective-permute-start.3) | collective-permute-done | bytes 71712 | tf_op jit(solution)/shard_map/ppermute | solution.py:17
  39.3 3.2 %fusion.32 = (bf16[16,64,896]{2,1,0:T(8,128)(2,1)S(1)}, bf16[16,64,896]{2,1,0:T(8,128)(2,1)S(1)}, bf16[16,64,896]{2,1,0:T(8,128)(2,1)S(1)}, bf16[16,64,896]{2,1,...) fusion(bf16[24,64,896]{2,1,0:T(8,128)(2,1)S(1)} %slice_dynamic-, ...), kind=kLoop, calls=%fused_computation.75 | loop fusion | bytes 33030144 | tf_op jit(solution)/shard_map/slice | solution.py:72
  48.3 0.9 broadcast_select_fusion
  49.2 10.2 %all-to-all-start = ((f32[16,1,64,128]{3,2,1,0:T(8,128)}), f32[16,1,64,128]{3,2,1,0:T(8,128)S(1)}, u32[]{:S(2)}, u32[]{:S(2)}) async-start(f32[16,1,64,128]{3,2,1,0:T(8,128)} %broadcast_select_fusion), calls=%async_computation | async-start | bytes 1048576 | tf_op jit(solution)/shard_map/all_to_all | solution.py:119
  59.4 17.3 %all-to-all-done = f32[16,1,64,128]{3,2,1,0:T(8,128)S(1)} async-done(((f32[16,1,64,128]{3,2,1,0:T(8,128)}), f32[16,1,64,128]{3,2,1,0:T(8,128)S(1)}, u32[]{:S(2)}, u32[]{:S(2)}) %all-to-all-start) | async-done | bytes 524320 | tf_op jit(solution)/shard_map/all_to_all | solution.py:119
  76.8 0.9 fusion.23
  77.7 31.3 %all_to_all.10 = f32[16,1,128,128]{3,2,1,0:T(8,128)S(1)} all-to-all(f32[16,1,128,128]{3,2,1,0:T(8,128)S(1)} %stack.2), channel_id=1, replica_groups=mesh['view'=16,'blk'=16] {'view'}, dimensions={0} | all-to-all | bytes 2097152 | tf_op jit(solution)/shard_map/all_to_all | solution.py:125
  109.0 1.0 copy.70
  (69 shorter events, 13.5 us)
Async XLA Ops:
  1.3 12.7 %collective-permute-start = (bf16[4,128,128]{2,1,0:T(8,128)(2,1)S(1)}, bf16[4,128,128]{2,1,0:T(8,128)(2,1)S(1)}, u32[]{:S(2)}, u32[]{:S(2)}) collective-permute-start(bf16[4,128,128]{2,1,0:T(8,128)(2,1)S(1)} %get-tuple-element.44), channel_id=1, source_target_pairs={{0,1},{1,2},{2,3},{3,4},{4,5},{5,6},{6,7},{7,8},{8,9},{9,10},{10,1... | collective-permute-start | bytes 393224 | tf_op jit(solution)/shard_map/ppermute | solution.py:17
  4.5 9.6 %collective-permute-start.1 = (bf16[4,128,128]{2,1,0:T(8,128)(2,1)S(1)}, bf16[4,128,128]{2,1,0:T(8,128)(2,1)S(1)}, u32[]{:S(2)}, u32[]{:S(2)}) collective-permute-start(bf16[4,128,128]{2,1,0:T(8,128)(2,1)S(1)} %get-tuple-element.43), channel_id=1, source_target_pairs={{1,0},{2,1},{3,2},{4,3},{5,4},{6,5},{7,6},{8,7},{9,8},{10,9},{11,1... | collective-permute-start | bytes 393224 | tf_op jit(solution)/shard_map/ppermute | solution.py:19
  12.2 0.7 copy-start.1
  24.0 1.0 copy-start
  25.1 2.2 %collective-permute-start.2 = (bf16[16,3,128]{2,1,0:T(4,128)(2,1)S(1)}, bf16[16,3,128]{2,1,0:T(4,128)(2,1)S(1)}, u32[]{:S(2)}, u32[]{:S(2)}) collective-permute-start(bf16[16,3,128]{2,1,0:T(4,128)(2,1)S(1)} %slice_select_fusion), channel_id=1, source_target_pairs={{0,16},{16,0},{32,48},{48,32},{64,80},{80,64},{96,112},{112,96},{1... | collective-permute-start | bytes 36872 | tf_op jit(solution)/shard_map/ppermute | solution.py:33
  27.4 6.1 %collective-permute-start.4 = (bf16[4,70,128]{2,1,0:T(8,128)(2,1)S(1)}, bf16[4,70,128]{2,1,0:T(8,128)(2,1)S(1)}, u32[]{:S(2)}, u32[]{:S(2)}) collective-permute-start(bf16[4,70,128]{2,1,0:T(8,128)(2,1)S(1)} %get-tuple-element.46), channel_id=1, source_target_pairs={{1,0},{2,1},{3,2},{4,3},{5,4},{6,5},{7,6},{8,7},{9,8},{10,9},{11,1... | collective-permute-start | bytes 215048 | tf_op jit(solution)/shard_map/ppermute | solution.py:19
  30.8 7.2 %collective-permute-start.3 = (bf16[4,70,128]{2,1,0:T(8,128)(2,1)S(1)}, bf16[4,70,128]{2,1,0:T(8,128)(2,1)S(1)}, u32[]{:S(2)}, u32[]{:S(2)}) collective-permute-start(bf16[4,70,128]{2,1,0:T(8,128)(2,1)S(1)} %get-tuple-element.45), channel_id=1, source_target_pairs={{0,1},{1,2},{2,3},{3,4},{4,5},{5,6},{6,7},{7,8},{8,9},{9,10},{10,1... | collective-permute-start | bytes 215048 | tf_op jit(solution)/shard_map/ppermute | solution.py:17
  49.2 27.5 %all-to-all-start = ((f32[16,1,64,128]{3,2,1,0:T(8,128)}), f32[16,1,64,128]{3,2,1,0:T(8,128)S(1)}, u32[]{:S(2)}, u32[]{:S(2)}) async-start(f32[16,1,64,128]{3,2,1,0:T(8,128)} %broadcast_select_fusion), calls=%async_computation | async-start | bytes 1048576 | tf_op jit(solution)/shard_map/all_to_all | solution.py:119
